TPU v7x, 512 devices: a whole 4x4x16 slice. The times are simulated.
512 devices in a mesh: along: 32 (over y, x, z_hi), cross: 16 (over z_lo, core).
Axes of the slice: x: 4, y: 4, z: 16 (z_hi: 2, z_lo: 8; z = z_hi * 8 + z_lo), core: 2. Of those that a mesh axis runs over, the one named last changes fastest.
Arguments:
- nadir_view: bfloat16 [8192, 24576], P('along', 'cross'), may hold values from -36 to 36
- forward: bfloat16 [8192, 24576], P('along', 'cross'), may hold values from -36 to 36
- backward: bfloat16 [8192, 24576], P('along', 'cross'), may hold values from -36 to 36
- along_weights: bfloat16 [2, 4, 8192], replicated, may hold values from 0.049804688 to 0.5
- cross_weights: bfloat16 [2, 4, 24576], P(None, None, 'cross'), may hold values from 0.049804688 to 0.5
- band_offsets: int32 [2, 8192], replicated, may hold values from -6 to 6, as said below
- col_offsets: int32 [2, 24576], P(None, 'cross'), may hold values from -6 to 6, as said below
- lag_lines: int32 [8192], replicated, may hold values from 20480 to 20495, as said below
- window_start: int32 [1], replicated, may hold values from 0 to 2088960
Outputs:
- parallax: bfloat16 [2, 8192, 24576], P(None, 'along', 'cross')
- normal_gram: float32 [32, 256, 256], P('along', 'cross')
- normal_rhs: float32 [32, 256], P('along', 'cross')
Inputs may be any that keep to these rules, and one draw needn't show every extreme that they name: `lag_lines`: every value in the range occurs in each draw. `band_offsets`: both ends of the range occur in each draw. `col_offsets`: both ends of the range occur in each draw.
All inputs are finite; a program needn't handle non-finite values.
Results may differ from a plain program's by a relative error of at most 0.0065.
Values may be sent and summed in bfloat16 or wider, within the bound.
A program may use at most 64 MiB of HBM per device.

v0:
```python
import jax
import jax.numpy as jnp
from jax import lax
from jax.sharding import PartitionSpec as P

TAPS = 4
CAMERA_LAG = 20480
BOX = 4
MODES = 64
LINE_RIM = 32
COL_RIM = 9


def shifted(value, axis, steps):
    count = lax.axis_size(axis)
    pairs = [(source, (source + steps) % count) for source in range(count)]
    return lax.ppermute(value, axis, pairs)


def extended(cells, sides, width):
    for axis, dim in sides:
        count = lax.axis_size(axis)
        ends = count - 1
        head = lax.slice_in_dim(cells, 0, width, axis=dim)
        tail = lax.slice_in_dim(cells, cells.shape[dim] - width, cells.shape[dim], axis=dim)
        cells = jnp.concatenate(
            [
                lax.ppermute(tail, axis, [(i, (i + 1) % count) for i in range(ends)]),
                cells,
                lax.ppermute(head, axis, [((i + 1) % count, i) for i in range(ends)]),
            ],
            axis=dim,
        )
    return cells


def harmonics(absolute):
    period = 4 * MODES
    factor = 2 * jnp.arange(MODES, dtype=jnp.int32) + 1
    phases = (absolute % period)[:, None] * factor[None, :] % period
    angles = phases.astype(jnp.float32) * (2.0 * jnp.pi / period)
    return jnp.concatenate([jnp.cos(angles), jnp.sin(angles)], axis=1)


def box_mean(values, count):
    running = values[0:count]
    for offset in range(1, 2 * BOX + 1):
        running = running + values[offset : offset + count]
    return running / (2 * BOX + 1)


def shift_slabs(lead_part, trail_part, distance):
    lead_moved = shifted(lead_part, "along", distance)
    trail_moved = shifted(trail_part, "along", -distance)
    return (lead_moved, trail_moved)


def line_margin(stacked):
    height = stacked.shape[1]
    from_below = shifted(stacked[:, height - LINE_RIM :], "along", 1)
    from_above = shifted(stacked[:, :LINE_RIM], "along", -1)
    return jnp.concatenate([from_below, stacked, from_above], axis=1)


def column_margin(stacked):
    return extended(stacked, (("cross", 2),), COL_RIM)


def margins(stacked):
    return column_margin(line_margin(stacked))


def along_resample(slab_ext, tap_weights, row_start):
    positions = jnp.arange(slab_ext.shape[0], dtype=jnp.int32)
    distance = positions[None, :] - row_start[:, None]
    banded = jnp.zeros(distance.shape, jnp.bfloat16)
    for tap_index in range(TAPS):
        banded = jnp.where(distance == tap_index, tap_weights[tap_index][:, None], banded)
    return jnp.dot(banded, slab_ext, preferred_element_type=jnp.float32).astype(jnp.bfloat16)


def cross_resample(along_ext, tap_weights, col_shift):
    out_width = col_shift.shape[0]
    tile_count = out_width // 128
    window = 128 + 2 * COL_RIM
    positions = jnp.arange(window, dtype=jnp.int32)
    starts = (
        COL_RIM + jnp.arange(128, dtype=jnp.int32)[None, :] + col_shift.reshape(tile_count, 128)
    )
    distance = positions[None, :, None] - starts[:, None, :]
    banded = jnp.zeros(distance.shape, jnp.bfloat16)
    for tap_index in range(TAPS):
        banded = jnp.where(
            distance == tap_index, tap_weights[tap_index].reshape(tile_count, 1, 128), banded
        )
    pieces = jnp.stack(
        [
            along_ext[:, tile_index * 128 : tile_index * 128 + window]
            for tile_index in range(tile_count)
        ]
    )
    product = jnp.einsum("qla,qaj->lqj", pieces, banded, preferred_element_type=jnp.float32)
    return product.reshape(along_ext.shape[0], out_width).astype(jnp.bfloat16)


def local(
    nadir_view,
    forward,
    backward,
    along_weights,
    cross_weights,
    band_offsets,
    col_offsets,
    lag_lines,
    window_start,
):
    lines_dev, cols_dev = nadir_view.shape
    along_count = lax.axis_size("along")
    cross_count = lax.axis_size("cross")
    along_index = lax.axis_index("along")
    cross_index = lax.axis_index("cross")
    total_lines = lines_dev * along_count
    total_cols = cols_dev * cross_count
    lag_blocks = along_count // 2
    lag_floor = CAMERA_LAG // total_lines * total_lines + lag_blocks * lines_dev
    lead_moved, trail_moved = shift_slabs(forward, backward, lag_blocks)
    widened = margins(jnp.stack([nadir_view, lead_moved, trail_moved]))
    nadir_full, lead_full, trail_full = (widened[0], widened[1], widened[2])
    local_lines = jnp.arange(-BOX, lines_dev + BOX, dtype=jnp.int32)
    wrapped = (along_index * lines_dev + local_lines) % total_lines
    lag_excess = jnp.take(lag_lines, wrapped) - lag_floor
    lead_start = LINE_RIM + local_lines - lag_excess + jnp.take(band_offsets[0], wrapped)
    trail_start = LINE_RIM + local_lines + lag_excess + jnp.take(band_offsets[1], wrapped)
    lead_along = along_resample(lead_full, jnp.take(along_weights[0], wrapped, axis=1), lead_start)
    trail_along = along_resample(
        trail_full, jnp.take(along_weights[1], wrapped, axis=1), trail_start
    )
    lead_res = cross_resample(lead_along, cross_weights[0], col_offsets[0])
    trail_res = cross_resample(trail_along, cross_weights[1], col_offsets[1])
    framed = nadir_full[
        LINE_RIM - BOX - 1 : LINE_RIM + lines_dev + BOX + 1, COL_RIM - 1 : COL_RIM + cols_dev + 1
    ].astype(jnp.float32)
    slopes = (
        framed[2:, :-2]
        + 2.0 * framed[2:, 1:-1]
        + framed[2:, 2:]
        - framed[:-2, :-2]
        - 2.0 * framed[:-2, 1:-1]
        - framed[:-2, 2:]
    ) / 4.0
    center = framed[1:-1, 1:-1]
    texture = box_mean(slopes * slopes, lines_dev)
    divisor = jnp.maximum(texture, 0.4)
    lead_est = -box_mean(slopes * (lead_res.astype(jnp.float32) - center), lines_dev) / divisor
    trail_est = -box_mean(slopes * (trail_res.astype(jnp.float32) - center), lines_dev) / divisor
    parallax = jnp.stack([lead_est, trail_est]).astype(jnp.bfloat16)
    disagree = lead_est + trail_est
    columns = cross_index * cols_dev + jnp.arange(cols_dev, dtype=jnp.int32)
    position = (columns.astype(jnp.float32) + 0.5) / total_cols + 0.25
    lever_two = position * position
    lever_three = lever_two * position
    lever_four = lever_two * lever_two
    scale_sum = 1.0 / (lines_dev * total_cols)
    scale_pull = 1.0 / (lines_dev * total_cols) ** 0.5
    line_terms = jnp.stack(
        [
            jnp.sum(texture * lever_two[None, :], axis=1) * scale_sum,
            jnp.sum(texture * lever_three[None, :], axis=1) * scale_sum,
            jnp.sum(texture * lever_four[None, :], axis=1) * scale_sum,
            jnp.sum(texture * disagree * position[None, :], axis=1) * scale_pull,
            jnp.sum(texture * disagree * lever_two[None, :], axis=1) * scale_pull,
        ]
    )
    basis_lines = harmonics(
        window_start[0] + along_index * lines_dev + jnp.arange(lines_dev, dtype=jnp.int32)
    )

    def weighted(coefs):
        return jnp.dot(
            (basis_lines * coefs[:, None]).T, basis_lines, precision=lax.Precision.HIGHEST
        )

    gram_part = jnp.concatenate(
        [
            jnp.concatenate([weighted(line_terms[0]), weighted(line_terms[1])], axis=1),
            jnp.concatenate([weighted(line_terms[1]), weighted(line_terms[2])], axis=1),
        ],
        axis=0,
    )
    rhs_part = jnp.concatenate(
        [
            jnp.dot(basis_lines.T, line_terms[3], precision=lax.Precision.HIGHEST),
            jnp.dot(basis_lines.T, line_terms[4], precision=lax.Precision.HIGHEST),
        ]
    )
    normal_gram, normal_rhs = (
        lax.psum_scatter(gram_part[None], "cross", scatter_dimension=1, tiled=True),
        lax.psum_scatter(rhs_part[None], "cross", scatter_dimension=1, tiled=True),
    )
    return (parallax, normal_gram, normal_rhs)


def solution(mesh):
    placed = (
        P("along", "cross"),
        P("along", "cross"),
        P("along", "cross"),
        P(),
        P(None, None, "cross"),
        P(),
        P(None, "cross"),
        P(),
        P(),
    )
    return jax.shard_map(
        local,
        mesh=mesh,
        in_specs=placed,
        out_specs=(P(None, "along", "cross"), P("along", "cross", None), P("along", "cross")),
        check_vma=False,
    )
```

profile of v0, /device:TPU:1, one launch (start us, length us, event | category | flops | bytes accessed | tf_op | source)
XLA Modules:
  0.0 458.3 jit_solution(1826869938773107744)
XLA Ops:
  7.2 5.6 %collective-permute-start = (bf16[256,1536]{1,0:T(8,128)(2,1)}, bf16[256,1536]{1,0:T(8,128)(2,1)S(1)}, u32[]{:S(2)}, u32[]{:S(2)}) collective-permute-start(bf16[256,1536]{1,0:T(8,128)(2,1)} %param.14), channel_id=1, source_target_pairs={{0,256},{16,272},{32,288},{48,304},{64,320},{80,336},{96,352},{112... | collective-permute-start | bytes 2359304 | tf_op jit(solution)/shard_map/ppermute | solution.py:17
  12.9 1.9 collective-permute-start.1
  15.8 1.9 copy.36
  17.7 1.9 copy.37
  19.6 2.9 gather_fusion.2
  22.5 2.9 gather_fusion.4
  25.5 2.2 gather_fusion.1
  27.8 2.2 gather_fusion.3
  30.1 2.2 gather_fusion
  34.5 9.5 %collective-permute-done.1 = bf16[256,1536]{1,0:T(8,128)(2,1)S(1)} collective-permute-done((bf16[256,1536]{1,0:T(8,128)(2,1)}, bf16[256,1536]{1,0:T(8,128)(2,1)S(1)}, u32[]{:S(2)}, u32[]{:S(2)}) %collective-permute-start.1) | collective-permute-done | bytes 786464 | tf_op jit(solution)/shard_map/ppermute | solution.py:17
  44.1 18.3 %collective-permute-start.2 = (bf16[3,32,1536]{2,1,0:T(8,128)(2,1)S(1)}, bf16[3,32,1536]{2,1,0:T(8,128)(2,1)S(1)}, u32[]{:S(2)}, u32[]{:S(2)}) collective-permute-start(bf16[3,32,1536]{2,1,0:T(8,128)(2,1)S(1)} %get-tuple-element.45), channel_id=1, source_target_pairs={{0,16},{16,32},{32,48},{48,64},{64,80},{80,96},{96,112},{112,128},... | collective-permute-start | bytes 884744 | tf_op jit(solution)/shard_map/ppermute | solution.py:17
  62.4 6.6 %collective-permute-start.3 = (bf16[3,32,1536]{2,1,0:T(8,128)(2,1)S(1)}, bf16[3,32,1536]{2,1,0:T(8,128)(2,1)S(1)}, u32[]{:S(2)}, u32[]{:S(2)}) collective-permute-start(bf16[3,32,1536]{2,1,0:T(8,128)(2,1)S(1)} %get-tuple-element.46), channel_id=1, source_target_pairs={{0,496},{16,0},{32,16},{48,32},{64,48},{80,64},{96,80},{112,96},{1... | collective-permute-start | bytes 884744 | tf_op jit(solution)/shard_map/ppermute | solution.py:17
  69.0 3.9 collective-permute-done.2
  72.9 14.3 %collective-permute-done.3 = bf16[3,32,1536]{2,1,0:T(8,128)(2,1)S(1)} collective-permute-done((bf16[3,32,1536]{2,1,0:T(8,128)(2,1)S(1)}, bf16[3,32,1536]{2,1,0:T(8,128)(2,1)S(1)}, u32[]{:S(2)}, u32[]{:S(2)}) %collective-permute-start.3) | collective-permute-done | bytes 294944 | tf_op jit(solution)/shard_map/ppermute | solution.py:17
  89.5 29.6 %collective-permute-start.4 = (bf16[3,320,9]{2,1,0:T(8,128)(2,1)}, bf16[3,320,9]{2,1,0:T(8,128)(2,1)S(1)}, u32[]{:S(2)}, u32[]{:S(2)}) collective-permute-start(bf16[3,320,9]{2,1,0:T(8,128)(2,1)} %get-tuple-element.44), channel_id=1, source_target_pairs={{0,1},{1,2},{2,3},{3,4},{4,5},{5,6},{6,7},{7,8},{8,9},{9,10},{10,1... | collective-permute-start | bytes 51848 | tf_op jit(solution)/shard_map/ppermute | solution.py:28
  119.2 2.1 collective-permute-start.5
  123.3 3.8 collective-permute-done.5
  127.0 6.0 %concatenate.22 = bf16[3,320,1554]{2,1,0:T(8,128)(2,1)} concatenate(bf16[3,320,9]{2,1,0:T(8,128)(2,1)S(1)} %collective-permute-done.4, bf16[3,320,1536]{2,1,0:T(8,128)(2,1)S(1)} %pad_maximum_fusion, bf16[3,320,9]{2,1,0:T(8,128)(2,1)} %collective-permute-done.5), dimensions={2} | concatenate | bytes 5967360 | tf_op jit(solution)/shard_map/concatenate | solution.py:26
  134.3 2.0 convolution_convert_fusion
  136.6 2.0 convolution_convert_fusion.1
  139.9 2.2 fusion.1
  143.4 4.7 %multiply_reduce_fusion.1 = (f32[256]{0:T(256)S(1)}, f32[256]{0:T(256)S(1)}, f32[256]{0:T(256)S(1)}, f32[256]{0:T(256)S(1)}, f32[256]{0:T(256)S(1)}, /*index=5*/...) fusion(f32[1536]{0:T(1024)S(1)} %get-tuple-element.65, f32[1536]{0:T(1024)S(1)} %get-tuple-element.66, ...), kind=kLoop, calls=%fused_computation.54 | loop fusion | flops 18086656 | bytes 44076032 | tf_op jit(solution)/shard_map/reduce_sum | solution.py:170
  152.9 96.0 %reduce-scatter.4.cloned.1.call-done = f32[16,1]{1,0:T(8,128)} async-done(((f32[256,1]{1,0:T(8,128)}), f32[16,1]{1,0:T(8,128)}) %reduce-scatter.4.cloned.1.call-update) | async-done | bytes 80
  250.2 200.0 %all-reduce.3.cloned.1.call-done = f32[1,256,256]{2,0,1:T(1,128)} async-done(((f32[1,256,256]{2,0,1:T(1,128)}), f32[1,256,256]{2,0,1:T(1,128)}) %all-reduce.3.cloned.1.call-update) | async-done | bytes 262160
  (92 shorter events, 17.5 us)
Async XLA Ops:
  7.2 22.9 %copy-start = (s32[8192]{0:T(1024)S(1)}, s32[8192]{0:T(1024)}, u32[]{:S(2)}) copy-start(s32[8192]{0:T(1024)} %param.20) | copy-start | bytes 98308
  7.2 241.8 %reduce-scatter.4.cloned.1.call-start = ((), (), s32[]{:S(2)}) async-start(), calls=%async_computation.1 | async-start | bytes 139264
  7.2 27.3 %collective-permute-start = (bf16[256,1536]{1,0:T(8,128)(2,1)}, bf16[256,1536]{1,0:T(8,128)(2,1)S(1)}, u32[]{:S(2)}, u32[]{:S(2)}) collective-permute-start(bf16[256,1536]{1,0:T(8,128)(2,1)} %param.14), channel_id=1, source_target_pairs={{0,256},{16,272},{32,288},{48,304},{64,320},{80,336},{96,352},{112... | collective-permute-start | bytes 2359304 | tf_op jit(solution)/shard_map/ppermute | solution.py:17
  12.9 31.2 %collective-permute-start.1 = (bf16[256,1536]{1,0:T(8,128)(2,1)}, bf16[256,1536]{1,0:T(8,128)(2,1)S(1)}, u32[]{:S(2)}, u32[]{:S(2)}) collective-permute-start(bf16[256,1536]{1,0:T(8,128)(2,1)} %param.15), channel_id=1, source_target_pairs={{0,256},{16,272},{32,288},{48,304},{64,320},{80,336},{96,352},{112... | collective-permute-start | bytes 2359304 | tf_op jit(solution)/shard_map/ppermute | solution.py:17
  17.7 7.8 %copy-start.6 = (s32[2,8192]{1,0:T(2,128)S(1)}, s32[2,8192]{1,0:T(2,128)}, u32[]{:S(2)}) copy-start(s32[2,8192]{1,0:T(2,128)} %param.18) | copy-start | bytes 196612
  27.8 4.5 copy-start.7
  30.0 3.7 copy-start.5
  30.1 14.0 %copy-start.1 = (bf16[256,1536]{1,0:T(8,128)(2,1)S(1)}, bf16[256,1536]{1,0:T(8,128)(2,1)}, u32[]{:S(2)}) copy-start(bf16[256,1536]{1,0:T(8,128)(2,1)} %param.13) | copy-start | bytes 2359300
  34.5 52.7 %copy-start.2 = (bf16[256,1536]{1,0:T(8,128)(2,1)S(1)}, bf16[256,1536]{1,0:T(8,128)(2,1)}, u32[]{:S(2)}) copy-start(bf16[256,1536]{1,0:T(8,128)(2,1)} %param.13) | copy-start | bytes 2359300
  34.5 38.4 %copy-start.3 = (bf16[256,1536]{1,0:T(8,128)(2,1)}, bf16[256,1536]{1,0:T(8,128)(2,1)S(1)}, u32[]{:S(2)}) copy-start(bf16[256,1536]{1,0:T(8,128)(2,1)S(1)} %collective-permute-done) | copy-start | bytes 2359300
  44.1 28.8 %copy-start.4 = (bf16[256,1536]{1,0:T(8,128)(2,1)}, bf16[256,1536]{1,0:T(8,128)(2,1)S(1)}, u32[]{:S(2)}) copy-start(bf16[256,1536]{1,0:T(8,128)(2,1)S(1)} %collective-permute-done.1) | copy-start | bytes 2359300
  44.1 28.8 %collective-permute-start.2 = (bf16[3,32,1536]{2,1,0:T(8,128)(2,1)S(1)}, bf16[3,32,1536]{2,1,0:T(8,128)(2,1)S(1)}, u32[]{:S(2)}, u32[]{:S(2)}) collective-permute-start(bf16[3,32,1536]{2,1,0:T(8,128)(2,1)S(1)} %get-tuple-element.45), channel_id=1, source_target_pairs={{0,16},{16,32},{32,48},{48,64},{64,80},{80,96},{96,112},{112,128},... | collective-permute-start | bytes 884744 | tf_op jit(solution)/shard_map/ppermute | solution.py:17
  62.4 24.8 %collective-permute-start.3 = (bf16[3,32,1536]{2,1,0:T(8,128)(2,1)S(1)}, bf16[3,32,1536]{2,1,0:T(8,128)(2,1)S(1)}, u32[]{:S(2)}, u32[]{:S(2)}) collective-permute-start(bf16[3,32,1536]{2,1,0:T(8,128)(2,1)S(1)} %get-tuple-element.46), channel_id=1, source_target_pairs={{0,496},{16,0},{32,16},{48,32},{64,48},{80,64},{96,80},{112,96},{1... | collective-permute-start | bytes 884744 | tf_op jit(solution)/shard_map/ppermute | solution.py:17
  89.5 33.7 %collective-permute-start.4 = (bf16[3,320,9]{2,1,0:T(8,128)(2,1)}, bf16[3,320,9]{2,1,0:T(8,128)(2,1)S(1)}, u32[]{:S(2)}, u32[]{:S(2)}) collective-permute-start(bf16[3,320,9]{2,1,0:T(8,128)(2,1)} %get-tuple-element.44), channel_id=1, source_target_pairs={{0,1},{1,2},{2,3},{3,4},{4,5},{5,6},{6,7},{7,8},{8,9},{9,10},{10,1... | collective-permute-start | bytes 51848 | tf_op jit(solution)/shard_map/ppermute | solution.py:28
  119.2 7.8 %collective-permute-start.5 = (bf16[3,320,9]{2,1,0:T(8,128)(2,1)}, bf16[3,320,9]{2,1,0:T(8,128)(2,1)}, u32[]{:S(2)}, u32[]{:S(2)}) collective-permute-start(bf16[3,320,9]{2,1,0:T(8,128)(2,1)} %get-tuple-element.43), channel_id=1, source_target_pairs={{1,0},{2,1},{3,2},{4,3},{5,4},{6,5},{7,6},{8,7},{9,8},{10,9},{11,1... | collective-permute-start | bytes 51848 | tf_op jit(solution)/shard_map/ppermute | solution.py:30
  149.4 300.8 %all-reduce.3.cloned.1.call-start = ((), (), s32[]{:S(2)}) async-start(), calls=%async_computation.2 | async-start | bytes 524288
Sparse Core Ops, SparseCore 0:
  149.5 99.4 reduce-scatter.3
  251.8 198.2 all-reduce.2
where the time goes:
time: 459 us; the launch traced here: 458 us
  waiting for transfers between devices  327 us (71%)
  starting transfers between devices  64.3 us (14%)
  local copies, waits for them, and re-layouts  31.9 us (7%)
  between operations  16 us (3%)
  other arithmetic  11.8 us (3%)
  matrix products  6.97 us (2%)
    unnamed x4, waiting for transfers between devices  296 us
    ppermute x4, starting transfers between devices, shifted(): return lax.ppermute(value, axis, pairs)  32.4 us
    ppermute x1, starting transfers between devices, extended(): lax.ppermute(tail, axis, [(i, (i + 1) % count) for i in range(ends)])  29.6 us
    ppermute x4, waiting for transfers between devices, shifted(): return lax.ppermute(value, axis, pairs)  27.7 us
  transfers between devices with their start and end apart: 8, of which 6 were waited for; matrix products, arithmetic and copies ran while one was open for 5% of the time, Pallas kernels for 0%

commit v1 on v0

--- a/solution.py
+++ b/solution.py
@@ -1,6 +1,8 @@
 import jax
 import jax.numpy as jnp
 from jax import lax
+from jax.experimental import pallas as pl
+from jax.experimental.pallas import tpu as pltpu
 from jax.sharding import PartitionSpec as P
 
 TAPS = 4
@@ -68,6 +70,56 @@
 
 def margins(stacked):
     return column_margin(line_margin(stacked))
+
+
+def sum_kernel(terms_ref, out_ref, gathered, send_sem, recv_sem):
+    count = lax.axis_size("cross")
+    me = lax.axis_index("cross")
+    barrier = pltpu.get_barrier_semaphore()
+    for step in range(1, count):
+        pl.semaphore_signal(
+            barrier,
+            inc=1,
+            device_id={"cross": lax.rem(me + step, count)},
+            device_id_type=pl.DeviceIdType.MESH,
+        )
+    pl.semaphore_wait(barrier, count - 1)
+    copies = []
+    for step in range(1, count):
+        copies.append(
+            pltpu.make_async_remote_copy(
+                src_ref=terms_ref,
+                dst_ref=gathered.at[step],
+                send_sem=send_sem.at[step],
+                recv_sem=recv_sem.at[step],
+                device_id={"cross": lax.rem(me + step, count)},
+                device_id_type=pl.DeviceIdType.MESH,
+            )
+        )
+    for copy in copies:
+        copy.start()
+    for copy in copies:
+        copy.wait()
+    total = terms_ref[...]
+    for step in range(1, count):
+        total = total + gathered[step]
+    out_ref[...] = total
+
+
+def cross_sum(terms):
+    count = lax.axis_size("cross")
+    return pl.pallas_call(
+        sum_kernel,
+        out_shape=jax.ShapeDtypeStruct(terms.shape, terms.dtype),
+        in_specs=[pl.BlockSpec(memory_space=pltpu.VMEM)],
+        out_specs=pl.BlockSpec(memory_space=pltpu.VMEM),
+        scratch_shapes=[
+            pltpu.VMEM((count,) + terms.shape, terms.dtype),
+            pltpu.SemaphoreType.DMA((count,)),
+            pltpu.SemaphoreType.DMA((count,)),
+        ],
+        compiler_params=pltpu.CompilerParams(collective_id=0, has_side_effects=True),
+    )(terms)
 
 
 def along_resample(slab_ext, tap_weights, row_start):
@@ -175,28 +227,17 @@
         window_start[0] + along_index * lines_dev + jnp.arange(lines_dev, dtype=jnp.int32)
     )
 
-    def weighted(coefs):
-        return jnp.dot(
-            (basis_lines * coefs[:, None]).T, basis_lines, precision=lax.Precision.HIGHEST
-        )
-
-    gram_part = jnp.concatenate(
-        [
-            jnp.concatenate([weighted(line_terms[0]), weighted(line_terms[1])], axis=1),
-            jnp.concatenate([weighted(line_terms[1]), weighted(line_terms[2])], axis=1),
-        ],
-        axis=0,
-    )
-    rhs_part = jnp.concatenate(
-        [
-            jnp.dot(basis_lines.T, line_terms[3], precision=lax.Precision.HIGHEST),
-            jnp.dot(basis_lines.T, line_terms[4], precision=lax.Precision.HIGHEST),
-        ]
-    )
-    normal_gram, normal_rhs = (
-        lax.psum_scatter(gram_part[None], "cross", scatter_dimension=1, tiled=True),
-        lax.psum_scatter(rhs_part[None], "cross", scatter_dimension=1, tiled=True),
-    )
+    summed = cross_sum(jnp.concatenate([line_terms, jnp.zeros((3, lines_dev), jnp.float32)]))
+    rows_dev = 4 * MODES // cross_count
+    half = cross_index // (cross_count // 2)
+    first = (cross_index % (cross_count // 2)) * rows_dev
+    mine = lax.dynamic_slice_in_dim(basis_lines, first, rows_dev, axis=1)
+    weights = lax.dynamic_slice_in_dim(summed, half, 2, axis=0)
+    pull = lax.dynamic_slice_in_dim(summed, 3 + half, 1, axis=0)[0]
+    scaled = mine[:, None, :] * weights.T[:, :, None]
+    gram = jnp.einsum("gqm,gn->mqn", scaled, basis_lines, precision=lax.Precision.HIGHEST)
+    normal_gram = gram.reshape(1, rows_dev, 4 * MODES)
+    normal_rhs = jnp.sum(mine * pull[:, None], axis=0)[None]
     return (parallax, normal_gram, normal_rhs)
 
 

time: 459 us -> 164 us (0.36)
  waiting for transfers between devices: 327 us -> 31.7 us
  Pallas kernels: 0 us -> 15.4 us
  between operations: 16 us -> 2.05 us
    unnamed x4 -> x0, waiting for transfers between devices: 296 us -> none
    pallas_call x0 -> x1, Pallas kernels: none -> 15.4 us  [cross_sum(): pl.pallas_call(sum_kernel, out_shape=jax.ShapeDtypeStruct(terms.shape, te...]
  transfers between devices with their start and end apart: 8 -> 6, of which waited for: 6 -> 5; matrix products, arithmetic and copies ran while one was open for 5% -> 13% of each run, Pallas kernels for 0% -> 0%
where the time goes in v1:
time: 164 us; the launch traced here: 163 us
  starting transfers between devices  64.2 us (39%)
  waiting for transfers between devices  31.7 us (19%)
  local copies, waits for them, and re-layouts  31 us (19%)
  Pallas kernels  15.4 us (9%)
  other arithmetic  13 us (8%)
  matrix products  5.57 us (3%)
  between operations  2.05 us (1%)
    ppermute x4, starting transfers between devices, shifted(): return lax.ppermute(value, axis, pairs)  32.4 us
    ppermute x1, starting transfers between devices, extended(): lax.ppermute(tail, axis, [(i, (i + 1) % count) for i in range(ends)])  29.6 us
    ppermute x4, waiting for transfers between devices, shifted(): return lax.ppermute(value, axis, pairs)  26 us
    pallas_call x1, Pallas kernels, cross_sum(): pl.pallas_call(sum_kernel, out_shape=jax.ShapeDtypeStruct(terms.shape, te...  15.4 us
    concatenate x1, local copies, waits for them, and re-layouts, extended(): jnp.concatenate([lax.ppermute(tail, axis, [(i, (i + 1) % count) for i in...  5.96 us
    reduce_sum x1, other arithmetic, local(): jnp.sum(texture * disagree * lever_two[None, :], axis=1) * scale_pull  4.75 us
    unnamed x72, local copies, waits for them, and re-layouts  4.71 us
    ppermute x1, waiting for transfers between devices, extended(): lax.ppermute(head, axis, [((i + 1) % count, i) for i in range(ends)])  4.4 us
  transfers between devices with their start and end apart: 6, of which 5 were waited for; matrix products, arithmetic and copies ran while one was open for 13% of the time, Pallas kernels for 0%

profile of v1, /device:TPU:1, one launch (start us, length us, event | category | flops | bytes accessed | tf_op | source)
XLA Modules:
  0.0 162.9 jit_solution(647664281646281465)
XLA Ops:
  0.6 5.6 %collective-permute-start = (bf16[256,1536]{1,0:T(8,128)(2,1)}, bf16[256,1536]{1,0:T(8,128)(2,1)S(1)}, u32[]{:S(2)}, u32[]{:S(2)}) collective-permute-start(bf16[256,1536]{1,0:T(8,128)(2,1)} %param.14), channel_id=1, source_target_pairs={{0,256},{16,272},{32,288},{48,304},{64,320},{80,336},{96,352},{112... | collective-permute-start | bytes 2359304 | tf_op jit(solution)/shard_map/ppermute | solution.py:19
  6.3 1.9 %collective-permute-start.1 = (bf16[256,1536]{1,0:T(8,128)(2,1)}, bf16[256,1536]{1,0:T(8,128)(2,1)S(1)}, u32[]{:S(2)}, u32[]{:S(2)}) collective-permute-start(bf16[256,1536]{1,0:T(8,128)(2,1)} %param.15), channel_id=1, source_target_pairs={{0,256},{16,272},{32,288},{48,304},{64,320},{80,336},{96,352},{112... | collective-permute-start | bytes 2359304 | tf_op jit(solution)/shard_map/ppermute | solution.py:19
  9.2 1.9 %copy.27 = bf16[1,4,8192]{1,2,0:T(8,128)(2,1)} copy(bf16[1,4,8192]{2,1,0:T(4,128)(2,1)S(1)} %get-tuple-element.41) | data formatting | bytes 131072
  11.1 1.9 %copy.28 = bf16[1,4,8192]{1,2,0:T(8,128)(2,1)} copy(bf16[1,4,8192]{2,1,0:T(4,128)(2,1)S(1)} %get-tuple-element.40) | data formatting | bytes 131072
  13.0 2.9 %gather_fusion.2 = bf16[264,4]{1,0:T(8,128)(2,1)S(1)} fusion(bf16[4,8192]{0,1:T(8,128)(2,1)} %bitcast.175, s32[1024]{0:T(1024)S(1)} %pad_clamp_fusion), kind=kCustom, calls=%fused_computation.1.clone | custom fusion | bytes 5280 | tf_op jit(solution)/shard_map/jit(_take)/gather | solution.py:186
  16.0 2.9 %gather_fusion.4 = bf16[264,4]{1,0:T(8,128)(2,1)S(1)} fusion(bf16[4,8192]{0,1:T(8,128)(2,1)} %bitcast.176, s32[1024]{0:T(1024)S(1)} %pad_clamp_fusion), kind=kCustom, calls=%fused_computation.4.clone | custom fusion | bytes 5280 | tf_op jit(solution)/shard_map/jit(_take)/gather | solution.py:188
  19.0 2.2 %gather_fusion.1 = s32[264]{0:T(512)S(1)} fusion(s32[8192]{0:T(1024)S(1)} %bitcast.166, s32[1024]{0:T(1024)S(1)} %pad_clamp_fusion), kind=kCustom, calls=%fused_computation.2.clone | custom fusion | bytes 3168 | tf_op jit(solution)/shard_map/jit(_take)/gather | solution.py:184
  21.2 2.2 %gather_fusion.3 = s32[264]{0:T(512)S(1)} fusion(s32[8192]{0:T(1024)S(1)} %bitcast.165, s32[1024]{0:T(1024)S(1)} %pad_clamp_fusion), kind=kCustom, calls=%fused_computation.3.clone | custom fusion | bytes 3168 | tf_op jit(solution)/shard_map/jit(_take)/gather | solution.py:185
  23.5 2.2 %gather_fusion = s32[264]{0:T(512)S(1)} fusion(s32[8192]{0:T(1024)S(1)} %copy-done, s32[1024]{0:T(1024)S(1)} %pad_clamp_fusion), kind=kCustom, calls=%fused_computation.clone | custom fusion | bytes 3168 | tf_op jit(solution)/shard_map/jit(_take)/gather | solution.py:183
  29.0 8.5 %collective-permute-done.1 = bf16[256,1536]{1,0:T(8,128)(2,1)S(1)} collective-permute-done((bf16[256,1536]{1,0:T(8,128)(2,1)}, bf16[256,1536]{1,0:T(8,128)(2,1)S(1)}, u32[]{:S(2)}, u32[]{:S(2)}) %collective-permute-start.1) | collective-permute-done | bytes 786464 | tf_op jit(solution)/shard_map/ppermute | solution.py:19
  37.5 18.3 %collective-permute-start.2 = (bf16[3,32,1536]{2,1,0:T(8,128)(2,1)S(1)}, bf16[3,32,1536]{2,1,0:T(8,128)(2,1)S(1)}, u32[]{:S(2)}, u32[]{:S(2)}) collective-permute-start(bf16[3,32,1536]{2,1,0:T(8,128)(2,1)S(1)} %get-tuple-element.38), channel_id=1, source_target_pairs={{0,16},{16,32},{32,48},{48,64},{64,80},{80,96},{96,112},{112,128},... | collective-permute-start | bytes 884744 | tf_op jit(solution)/shard_map/ppermute | solution.py:19
  55.9 6.6 %collective-permute-start.3 = (bf16[3,32,1536]{2,1,0:T(8,128)(2,1)S(1)}, bf16[3,32,1536]{2,1,0:T(8,128)(2,1)S(1)}, u32[]{:S(2)}, u32[]{:S(2)}) collective-permute-start(bf16[3,32,1536]{2,1,0:T(8,128)(2,1)S(1)} %get-tuple-element.39), channel_id=1, source_target_pairs={{0,496},{16,0},{32,16},{48,32},{64,48},{80,64},{96,80},{112,96},{1... | collective-permute-start | bytes 884744 | tf_op jit(solution)/shard_map/ppermute | solution.py:19
  63.0 3.3 %collective-permute-done.2 = bf16[3,32,1536]{2,1,0:T(8,128)(2,1)S(1)} collective-permute-done((bf16[3,32,1536]{2,1,0:T(8,128)(2,1)S(1)}, bf16[3,32,1536]{2,1,0:T(8,128)(2,1)S(1)}, u32[]{:S(2)}, u32[]{:S(2)}) %collective-permute-start.2) | collective-permute-done | bytes 294944 | tf_op jit(solution)/shard_map/ppermute | solution.py:19
  66.3 14.3 %collective-permute-done.3 = bf16[3,32,1536]{2,1,0:T(8,128)(2,1)S(1)} collective-permute-done((bf16[3,32,1536]{2,1,0:T(8,128)(2,1)S(1)}, bf16[3,32,1536]{2,1,0:T(8,128)(2,1)S(1)}, u32[]{:S(2)}, u32[]{:S(2)}) %collective-permute-start.3) | collective-permute-done | bytes 294944 | tf_op jit(solution)/shard_map/ppermute | solution.py:19
  80.6 1.5 pad_maximum_fusion
  83.0 29.6 %collective-permute-start.4 = (bf16[3,320,9]{2,1,0:T(8,128)(2,1)}, bf16[3,320,9]{2,1,0:T(8,128)(2,1)S(1)}, u32[]{:S(2)}, u32[]{:S(2)}) collective-permute-start(bf16[3,320,9]{2,1,0:T(8,128)(2,1)} %get-tuple-element.37), channel_id=1, source_target_pairs={{0,1},{1,2},{2,3},{3,4},{4,5},{5,6},{6,7},{7,8},{8,9},{9,10},{10,1... | collective-permute-start | bytes 51848 | tf_op jit(solution)/shard_map/ppermute | solution.py:30
  112.6 2.1 %collective-permute-start.5 = (bf16[3,320,9]{2,1,0:T(8,128)(2,1)}, bf16[3,320,9]{2,1,0:T(8,128)(2,1)}, u32[]{:S(2)}, u32[]{:S(2)}) collective-permute-start(bf16[3,320,9]{2,1,0:T(8,128)(2,1)} %get-tuple-element.36), channel_id=1, source_target_pairs={{1,0},{2,1},{3,2},{4,3},{5,4},{6,5},{7,6},{8,7},{9,8},{10,9},{11,1... | collective-permute-start | bytes 51848 | tf_op jit(solution)/shard_map/ppermute | solution.py:32
  116.1 4.4 %collective-permute-done.5 = bf16[3,320,9]{2,1,0:T(8,128)(2,1)} collective-permute-done((bf16[3,320,9]{2,1,0:T(8,128)(2,1)}, bf16[3,320,9]{2,1,0:T(8,128)(2,1)}, u32[]{:S(2)}, u32[]{:S(2)}) %collective-permute-start.5) | collective-permute-done | bytes 17312 | tf_op jit(solution)/shard_map/ppermute | solution.py:32
  120.5 6.0 %concatenate.13 = bf16[3,320,1554]{2,1,0:T(8,128)(2,1)} concatenate(bf16[3,320,9]{2,1,0:T(8,128)(2,1)S(1)} %collective-permute-done.4, bf16[3,320,1536]{2,1,0:T(8,128)(2,1)S(1)} %pad_maximum_fusion, bf16[3,320,9]{2,1,0:T(8,128)(2,1)} %collective-permute-done.5), dimensions={2} | concatenate | bytes 5967360 | tf_op jit(solution)/shard_map/concatenate | solution.py:28
  127.8 2.0 %convolution_convert_fusion = bf16[264,1554]{1,0:T(8,128)(2,1)S(1)} fusion(bf16[3,320,1554]{2,1,0:T(8,128)(2,1)} %concatenate.13, s32[264]{0:T(512)S(1)} %copy-done.15, bf16[264]{0:T(512)(128)(2,1)S(1)} %copy-done.21, bf16[264]{0:T(512)(128)(2,1)S(1)} %copy-done.22, bf16[264]{0:T(512)(128)(2,1)S(1)} %copy-done.23, bf16[264]{0:T(512)(128)(2,1)S(1)} %copy-done.20), kind=kOutput, calls=%fused_computation.6 | convolution fusion | flops 263734416 | bytes 1888640 | tf_op jit(solution)/shard_map/dot_general | solution.py:131
  130.5 2.0 %convolution_convert_fusion.1 = bf16[264,1554]{1,0:T(8,128)(2,1)S(1)} fusion(bf16[3,320,1554]{2,1,0:T(8,128)(2,1)} %concatenate.13, s32[264]{0:T(512)S(1)} %copy-done.14, bf16[264]{0:T(512)(128)(2,1)S(1)} %copy-done.18, bf16[264]{0:T(512)(128)(2,1)S(1)} %copy-done.17, bf16[264]{0:T(512)(128)(2,1)S(1)} %copy-done.16, bf16[264]{0:T(512)(128)(2,1)S(1)} %copy-done.19), kind=kOutput, calls=%fused_computation.7 | convolution fusion | flops 263734416 | bytes 1888640 | tf_op jit(solution)/shard_map/dot_general | solution.py:131
  134.1 2.2 %fusion.1 = (f32[264,1536]{1,0:T(8,128)S(1)}, f32[264,1536]{1,0:T(8,128)S(1)}) fusion(f32[12,33,8,128]{3,2,1,0:T(8,128)S(1)} %convert_bitcast_fusion.1, f32[266,1538]{1,0:T(8,128)S(1)} %slice_convert_fusion), kind=kLoop, calls=%fused_computation.11 | loop fusion | flops 4055040 | bytes 16220160 | tf_op jit(solution)/shard_map/mul | solution.py:206
  137.6 4.8 %multiply_reduce_fusion = (f32[256]{0:T(256)S(1)}, f32[256]{0:T(256)S(1)}, f32[256]{0:T(256)S(1)}, f32[256]{0:T(256)S(1)}, f32[256]{0:T(256)S(1)}, /*index=5*/bf...) fusion(f32[1536]{0:T(1024)S(1)} %get-tuple-element.55, f32[1536]{0:T(1024)S(1)} %get-tuple-element.54, ...), kind=kLoop, calls=%fused_computation.53 | loop fusion | flops 18086656 | bytes 44076032 | tf_op jit(solution)/shard_map/reduce_sum | solution.py:223
  143.1 15.4 %shard_map.112 = f32[8,256]{1,0:T(8,128)} custom-call(f32[8,256]{1,0:T(8,128)} %concatenate.15.terms_ref), custom_call_target="tpu_custom_call" | custom-call | tf_op jit(solution)/shard_map/pallas_call | solution.py:111
  (115 shorter events, 16.0 us)
Async XLA Ops:
  0.6 22.9 %copy-start = (s32[8192]{0:T(1024)S(1)}, s32[8192]{0:T(1024)}, u32[]{:S(2)}) copy-start(s32[8192]{0:T(1024)} %param.20) | copy-start | bytes 98308
  0.6 28.4 %collective-permute-start = (bf16[256,1536]{1,0:T(8,128)(2,1)}, bf16[256,1536]{1,0:T(8,128)(2,1)S(1)}, u32[]{:S(2)}, u32[]{:S(2)}) collective-permute-start(bf16[256,1536]{1,0:T(8,128)(2,1)} %param.14), channel_id=1, source_target_pairs={{0,256},{16,272},{32,288},{48,304},{64,320},{80,336},{96,352},{112... | collective-permute-start | bytes 2359304 | tf_op jit(solution)/shard_map/ppermute | solution.py:19
  6.3 31.2 %collective-permute-start.1 = (bf16[256,1536]{1,0:T(8,128)(2,1)}, bf16[256,1536]{1,0:T(8,128)(2,1)S(1)}, u32[]{:S(2)}, u32[]{:S(2)}) collective-permute-start(bf16[256,1536]{1,0:T(8,128)(2,1)} %param.15), channel_id=1, source_target_pairs={{0,256},{16,272},{32,288},{48,304},{64,320},{80,336},{96,352},{112... | collective-permute-start | bytes 2359304 | tf_op jit(solution)/shard_map/ppermute | solution.py:19
  11.1 7.8 %copy-start.6 = (s32[2,8192]{1,0:T(2,128)S(1)}, s32[2,8192]{1,0:T(2,128)}, u32[]{:S(2)}) copy-start(s32[2,8192]{1,0:T(2,128)} %param.18) | copy-start | bytes 196612
  21.2 4.5 %copy-start.5 = (bf16[2,4,1536]{2,1,0:T(4,128)(2,1)S(1)}, bf16[2,4,1536]{2,1,0:T(4,128)(2,1)}, u32[]{:S(2)}) copy-start(bf16[2,4,1536]{2,1,0:T(4,128)(2,1)} %param.17) | copy-start | bytes 73732
  21.2 5.3 %copy-start.7 = (s32[2,1536]{1,0:T(2,128)S(1)}, s32[2,1536]{1,0:T(2,128)}, u32[]{:S(2)}) copy-start(s32[2,1536]{1,0:T(2,128)} %param.19) | copy-start | bytes 36868
  23.5 14.0 %copy-start.1 = (bf16[256,1536]{1,0:T(8,128)(2,1)S(1)}, bf16[256,1536]{1,0:T(8,128)(2,1)}, u32[]{:S(2)}) copy-start(bf16[256,1536]{1,0:T(8,128)(2,1)} %param.13) | copy-start | bytes 2359300
  29.0 51.6 %copy-start.2 = (bf16[256,1536]{1,0:T(8,128)(2,1)S(1)}, bf16[256,1536]{1,0:T(8,128)(2,1)}, u32[]{:S(2)}) copy-start(bf16[256,1536]{1,0:T(8,128)(2,1)} %param.13) | copy-start | bytes 2359300
  29.0 37.3 %copy-start.3 = (bf16[256,1536]{1,0:T(8,128)(2,1)}, bf16[256,1536]{1,0:T(8,128)(2,1)S(1)}, u32[]{:S(2)}) copy-start(bf16[256,1536]{1,0:T(8,128)(2,1)S(1)} %collective-permute-done) | copy-start | bytes 2359300
  37.5 28.8 %copy-start.4 = (bf16[256,1536]{1,0:T(8,128)(2,1)}, bf16[256,1536]{1,0:T(8,128)(2,1)S(1)}, u32[]{:S(2)}) copy-start(bf16[256,1536]{1,0:T(8,128)(2,1)S(1)} %collective-permute-done.1) | copy-start | bytes 2359300
  37.5 28.8 %collective-permute-start.2 = (bf16[3,32,1536]{2,1,0:T(8,128)(2,1)S(1)}, bf16[3,32,1536]{2,1,0:T(8,128)(2,1)S(1)}, u32[]{:S(2)}, u32[]{:S(2)}) collective-permute-start(bf16[3,32,1536]{2,1,0:T(8,128)(2,1)S(1)} %get-tuple-element.38), channel_id=1, source_target_pairs={{0,16},{16,32},{32,48},{48,64},{64,80},{80,96},{96,112},{112,128},... | collective-permute-start | bytes 884744 | tf_op jit(solution)/shard_map/ppermute | solution.py:19
  55.9 24.8 %collective-permute-start.3 = (bf16[3,32,1536]{2,1,0:T(8,128)(2,1)S(1)}, bf16[3,32,1536]{2,1,0:T(8,128)(2,1)S(1)}, u32[]{:S(2)}, u32[]{:S(2)}) collective-permute-start(bf16[3,32,1536]{2,1,0:T(8,128)(2,1)S(1)} %get-tuple-element.39), channel_id=1, source_target_pairs={{0,496},{16,0},{32,16},{48,32},{64,48},{80,64},{96,80},{112,96},{1... | collective-permute-start | bytes 884744 | tf_op jit(solution)/shard_map/ppermute | solution.py:19
  83.0 33.1 %collective-permute-start.4 = (bf16[3,320,9]{2,1,0:T(8,128)(2,1)}, bf16[3,320,9]{2,1,0:T(8,128)(2,1)S(1)}, u32[]{:S(2)}, u32[]{:S(2)}) collective-permute-start(bf16[3,320,9]{2,1,0:T(8,128)(2,1)} %get-tuple-element.37), channel_id=1, source_target_pairs={{0,1},{1,2},{2,3},{3,4},{4,5},{5,6},{6,7},{7,8},{8,9},{9,10},{10,1... | collective-permute-start | bytes 51848 | tf_op jit(solution)/shard_map/ppermute | solution.py:30
  112.6 7.8 %collective-permute-start.5 = (bf16[3,320,9]{2,1,0:T(8,128)(2,1)}, bf16[3,320,9]{2,1,0:T(8,128)(2,1)}, u32[]{:S(2)}, u32[]{:S(2)}) collective-permute-start(bf16[3,320,9]{2,1,0:T(8,128)(2,1)} %get-tuple-element.36), channel_id=1, source_target_pairs={{1,0},{2,1},{3,2},{4,3},{5,4},{6,5},{7,6},{8,7},{9,8},{10,9},{11,1... | collective-permute-start | bytes 51848 | tf_op jit(solution)/shard_map/ppermute | solution.py:32
  126.4 1.3 copy-start.15
  126.4 1.3 copy-start.20
  126.4 1.4 copy-start.21
  126.4 1.4 copy-start.22
  126.4 1.4 copy-start.23
  129.9 0.7 copy-start.18
  132.8 0.7 copy-start.10
  132.8 0.7 copy-start.11
  134.1 2.2 %copy-start.8 = (bf16[1536]{0:T(1024)(128)(2,1)S(1)}, bf16[1536]{0:T(1024)(128)(2,1)}, u32[]{:S(2)}) copy-start(bf16[1536]{0:T(1024)(128)(2,1)} %get-tuple-element.24) | copy-start | bytes 9220
  134.1 2.2 %copy-start.9 = (bf16[1536]{0:T(1024)(128)(2,1)S(1)}, bf16[1536]{0:T(1024)(128)(2,1)}, u32[]{:S(2)}) copy-start(bf16[1536]{0:T(1024)(128)(2,1)} %get-tuple-element.25) | copy-start | bytes 9220
  (6 other events, 4.0 us)
